TPU v7x, 32 devices: a whole 2x2x4 slice. The times are simulated.
32 devices in a mesh: rep: 8 (over z, x), shard: 4 (over y, core).
Axes of the slice: x: 2, y: 2, z: 4, core: 2. Of those that a mesh axis runs over, the one named last changes fastest.
Arguments:
- grads: bfloat16 [8, 12, 512, 512], P('rep', 'shard')
- owner_slot: int32 [12], replicated, may hold values from 0 to 11, as said below
- refresh: int32 [1], replicated, may hold values from 0 to 11
- left_stat: float32 [12, 512, 512], P('shard', 'rep'), as said below
- right_stat: float32 [12, 512, 512], P('shard', 'rep'), as said below
- left_root: bfloat16 [12, 512, 512], P('shard', 'rep'), as said below
- right_root: bfloat16 [12, 512, 512], P('shard'), as said below
Outputs:
- left_new: float32 [12, 512, 512], P('shard', 'rep')
- right_new: float32 [12, 512, 512], P('shard', 'rep')
- left_root_new: bfloat16 [12, 512, 512], P('shard', 'rep')
- right_root_new: bfloat16 [12, 512, 512], P('shard')
- direction: bfloat16 [12, 512, 512], P('shard')
Inputs may be any that keep to these rules, and one draw needn't show every extreme that they name: A permutation: block b sits at position owner_slot[b] of owner order, which belongs to shard index owner_slot[b] // 3, with owner_slot[b] % 3 == b % 3; the 3 blocks s * 3 to s * 3 + 2 all go to different shard indices. `left_stat`: each block is symmetric positive definite. `right_stat`: each block is symmetric positive definite. `left_root`: each block is symmetric. `right_root`: each block is symmetric.
All inputs are finite; a program needn't handle non-finite values.
Results may differ from a plain program's by a relative error of at most 0.0004.
The roundings to bfloat16 on the way count: a program that leaves them out, or rounds other values in their place, can miss the bound.
Values may be sent and summed in bfloat16 or wider, within the bound.
A program may use at most 64 MiB of HBM per device.

v0:
```python
import jax
import jax.numpy as jnp
from jax import lax
from jax.sharding import PartitionSpec as P

ITERS = 2
decay_rate = 0.95
epsilon_shift = 1e-06


def inverse_root(statistic):
    order = statistic.shape[0]
    identity = jnp.eye(order, dtype=jnp.float32)
    shifted = statistic + epsilon_shift * identity
    norm_scale = 2.5 / jnp.sqrt(jnp.sum(shifted * shifted))
    moment = norm_scale * shifted
    current = identity
    for number in range(ITERS):
        factor = (5.0 * identity - moment) * 0.25
        factor_low = factor.astype(jnp.bfloat16)
        if number == 0:
            current = jnp.sqrt(jnp.sqrt(norm_scale)) * factor
        else:
            current = jnp.dot(
                current.astype(jnp.bfloat16), factor_low, preferred_element_type=jnp.float32
            )
        if number + 1 < ITERS:
            square = jnp.dot(factor_low, factor_low, preferred_element_type=jnp.float32).astype(
                jnp.bfloat16
            )
            fourth = jnp.dot(square, square, preferred_element_type=jnp.float32).astype(
                jnp.bfloat16
            )
            moment = jnp.dot(
                fourth, moment.astype(jnp.bfloat16), preferred_element_type=jnp.float32
            )
    return current.astype(jnp.bfloat16)


def both_roots(fresh_whole):
    return (inverse_root(fresh_whole[0]), inverse_root(fresh_whole[1]))


def empty_roots(fresh_whole):
    blank = jnp.zeros(fresh_whole.shape[1:], jnp.bfloat16)
    return (blank, blank)


def body(grads, owner_slot, refresh, left_stat, right_stat, left_root, right_root):
    blocks = grads.shape[1]
    block_order = grads.shape[2]
    rep_count = lax.axis_size("rep")
    shards = lax.axis_size("shard")
    row_count = block_order // rep_count
    rep_index = lax.axis_index("rep")
    shard_index = lax.axis_index("shard")
    partial_value = grads[0].astype(jnp.float32)
    row_share = lax.psum_scatter(partial_value, "rep", scatter_dimension=1, tiled=True)
    row_share = row_share.astype(jnp.bfloat16)
    slot_table = owner_slot.reshape(shards, blocks)
    own_slots = lax.dynamic_index_in_dim(slot_table, shard_index, 0, keepdims=False)
    targets = own_slots // blocks
    selector = (targets[None, :] == jnp.arange(shards, dtype=jnp.int32)[:, None]).astype(
        jnp.bfloat16
    )
    outgoing = jnp.einsum(
        "ok,krc->orc", selector, row_share, preferred_element_type=jnp.float32
    ).astype(jnp.bfloat16)
    incoming = lax.all_to_all(outgoing, "shard", split_axis=0, concat_axis=0, tiled=True)
    wanted = shard_index * blocks + jnp.arange(blocks, dtype=jnp.int32)
    receiver = (jnp.transpose(slot_table) == wanted[:, None]).astype(jnp.bfloat16)
    owned_rows = jnp.einsum(
        "ks,src->krc", receiver, incoming, preferred_element_type=jnp.float32
    ).astype(jnp.bfloat16)
    gathered = lax.all_gather(owned_rows, "rep", axis=1, tiled=True)
    left_new = (
        decay_rate * left_stat
        + jnp.einsum("krc,kjc->krj", owned_rows, gathered, preferred_element_type=jnp.float32)
        / block_order
    )
    column_share = lax.dynamic_slice_in_dim(gathered, rep_index * row_count, row_count, 2)
    right_new = (
        decay_rate * right_stat
        + jnp.einsum("kic,kij->kcj", column_share, gathered, preferred_element_type=jnp.float32)
        / block_order
    )
    fresh_slot = owner_slot[refresh[0]]
    holder = fresh_slot // blocks
    slot_index = fresh_slot % blocks
    owns_fresh = holder == shard_index
    fresh_pair = jnp.stack(
        [
            lax.dynamic_index_in_dim(left_new, slot_index, 0, keepdims=False),
            lax.dynamic_index_in_dim(right_new, slot_index, 0, keepdims=False),
        ]
    )
    fresh_whole = lax.all_gather(fresh_pair, "rep", axis=1, tiled=True)
    fresh_left, fresh_right = lax.cond(owns_fresh, both_roots, empty_roots, fresh_whole)
    fresh_rows = lax.dynamic_slice_in_dim(fresh_left, rep_index * row_count, row_count, 0)
    left_updated = lax.dynamic_update_index_in_dim(left_root, fresh_rows, slot_index, 0)
    left_root_new = jnp.where(owns_fresh, left_updated, left_root)
    right_updated = lax.dynamic_update_index_in_dim(right_root, fresh_right, slot_index, 0)
    right_root_new = jnp.where(owns_fresh, right_updated, right_root)
    half_step = jnp.einsum(
        "kri,kic->krc", left_root_new, gathered, preferred_element_type=jnp.float32
    ).astype(jnp.bfloat16)
    preconditioned = jnp.einsum(
        "kri,kic->krc", half_step, right_root_new, preferred_element_type=jnp.float32
    ).astype(jnp.bfloat16)
    direction = lax.all_gather(preconditioned, "rep", axis=1, tiled=True)
    return (left_new, right_new, left_root_new, right_root_new, direction)


def solution(mesh):
    return jax.shard_map(
        body,
        mesh=mesh,
        in_specs=(
            P("rep", "shard", None, None),
            P(),
            P(),
            P("shard", "rep", None),
            P("shard", "rep", None),
            P("shard", "rep", None),
            P("shard", None, None),
        ),
        out_specs=(
            P("shard", "rep", None),
            P("shard", "rep", None),
            P("shard", "rep", None),
            P("shard", None, None),
            P("shard", None, None),
        ),
        check_vma=False,
    )
```

profile of v0, /device:TPU:0, one launch (start us, length us, event | category | flops | bytes accessed | tf_op | source)
XLA Modules:
  0.0 272.0 jit_solution(3963300385175303924)
XLA Ops:
  7.2 0.0 copy-start.3
  7.2 0.0 reduce-scatter.2.cloned.1.call-start
  7.2 1.4 copy-done.3
  8.6 2.1 bitcast_convert_fusion
  10.7 0.0 copy-start.10
  10.7 0.0 reduce-scatter.2.cloned.1.call-update
  10.7 0.6 copy-done.10
  11.3 0.1 reshape.53
  11.4 77.7 %reduce-scatter.2.cloned.1.call-done = f32[3,64,512]{2,1,0:T(8,128)} async-done(((f32[3,512,512]{2,1,0:T(8,128)}), f32[3,64,512]{2,1,0:T(8,128)}) %reduce-scatter.2.cloned.1.call-update) | async-done | bytes 393232 | tf_op jit(solution)/shard_map/reduce_scatter | solution.py:58
  89.1 1.0 convert_element_type.80
  90.1 0.0 copy-start.8
  90.2 0.3 convolution_convert_fusion.6
  90.4 0.7 copy.23
  91.2 3.4 %all-to-all-start = ((bf16[4,64,512]{2,1,0:T(8,128)(2,1)}), bf16[4,64,512]{2,1,0:T(8,128)(2,1)S(1)}, u32[]{:S(2)}, u32[]{:S(2)}) async-start(bf16[4,64,512]{2,1,0:T(8,128)(2,1)} %copy.23), calls=%async_computation.1 | async-start | bytes 524288 | tf_op jit(solution)/shard_map/all_to_all | solution.py:69
  94.6 0.0 all-gather.4.cloned.1.call-start
  94.7 5.9 %all-to-all-done = bf16[4,64,512]{2,1,0:T(8,128)(2,1)S(1)} async-done(((bf16[4,64,512]{2,1,0:T(8,128)(2,1)}), bf16[4,64,512]{2,1,0:T(8,128)(2,1)S(1)}, u32[]{:S(2)}, u32[]{:S(2)}) %all-to-all-start) | async-done | bytes 262176 | tf_op jit(solution)/shard_map/all_to_all | solution.py:69
  100.6 0.4 fusion.92
  100.9 0.0 copy-start.9
  101.0 0.7 copy.36
  101.7 0.0 all-gather.4.cloned.1.call-update
  101.7 0.0 all-gather.6.cloned.1.call-start
  102.4 0.6 dynamic_slice.22
  103.7 40.6 %all-gather.4.cloned.1.call-done = bf16[3,512,512]{2,1,0:T(8,128)(2,1)} async-done(((bf16[3,64,512]{2,1,0:T(8,128)(2,1)}), bf16[3,512,512]{2,1,0:T(8,128)(2,1)}) %all-gather.4.cloned.1.call-update) | async-done | bytes 1572880 | tf_op jit(solution)/shard_map/all_gather | solution.py:75
  144.2 0.0 copy-done.8
  144.2 0.0 copy-start
  144.2 2.2 fusion.90
  146.5 0.0 copy-done.9
  146.5 0.0 copy-done
  146.5 0.0 copy-start.6
  146.5 0.5 fusion.89
  147.0 0.2 copy-done.6
  147.2 0.0 copy-start.7
  147.2 0.7 copy-done.7
  148.0 0.7 pad_maximum_fusion
  148.7 0.0 all-gather.6.cloned.1.call-update
  148.7 0.0 all-gather.8.cloned.1.call-start
  150.1 0.0 copy-start.2
  150.1 46.2 %all-gather.6.cloned.1.call-done = f32[2,512,512]{2,1,0:T(8,128)} async-done(((f32[2,64,512]{2,1,0:T(8,128)}), f32[2,512,512]{2,1,0:T(8,128)}) %all-gather.6.cloned.1.call-update) | async-done | bytes 2097168 | tf_op jit(solution)/shard_map/all_gather | solution.py:97
  196.3 1.7 conditional.1
  196.3 0.8 broadcast.90
  197.1 0.8 broadcast_in_dim.12
  198.0 0.0 copy-start.5
  198.0 0.0 copy-done.2
  198.0 0.2 select_dynamic-update-slice_fusion
  198.1 0.0 copy-start.1
  198.2 0.7 copy-done.5
  198.9 0.9 fusion.95
  199.7 0.0 copy-start.4
  199.8 1.3 convolution_convert_fusion.7
  201.1 0.0 copy-done.1
  201.1 0.0 copy-done.4
  201.1 0.0 all-gather.8.cloned.1.call-update
  201.1 61.7 %all-gather.8.cloned.1.call-done = bf16[3,512,512]{2,1,0:T(8,128)(2,1)} async-done(((bf16[3,64,512]{2,1,0:T(8,128)(2,1)}), bf16[3,512,512]{2,1,0:T(8,128)(2,1)}) %all-gather.8.cloned.1.call-update) | async-done | bytes 1572880 | tf_op jit(solution)/shard_map/all_gather | solution.py:110
  262.8 2.7 copy.49
  (3 shorter events, 0.0 us)
Async XLA Ops:
  7.2 1.4 copy-start.3
  7.2 81.9 %reduce-scatter.2.cloned.1.call-start = ((), (), s32[]{:S(2)}) async-start(), calls=%async_computation.2 | async-start | bytes 3538944 | tf_op jit(solution)/shard_map/reduce_scatter | solution.py:58
  10.7 0.7 copy-start.10
  90.1 54.1 %copy-start.8 = (f32[3,64,512]{2,1,0:T(8,128)S(1)}, f32[3,64,512]{2,1,0:T(8,128)}, u32[]{:S(2)}) copy-start(f32[3,64,512]{2,1,0:T(8,128)} %param.12) | copy-start | bytes 1179652
  91.2 9.4 %all-to-all-start = ((bf16[4,64,512]{2,1,0:T(8,128)(2,1)}), bf16[4,64,512]{2,1,0:T(8,128)(2,1)S(1)}, u32[]{:S(2)}, u32[]{:S(2)}) async-start(bf16[4,64,512]{2,1,0:T(8,128)(2,1)} %copy.23), calls=%async_computation.1 | async-start | bytes 524288 | tf_op jit(solution)/shard_map/all_to_all | solution.py:69
  94.6 49.6 %all-gather.4.cloned.1.call-start = ((), (), s32[]{:S(2)}) async-start(), calls=%async_computation.3 | async-start | bytes 1769472 | tf_op jit(solution)/shard_map/all_gather | solution.py:75
  100.9 45.5 %copy-start.9 = (f32[3,64,512]{2,1,0:T(8,128)S(1)}, f32[3,64,512]{2,1,0:T(8,128)}, u32[]{:S(2)}) copy-start(f32[3,64,512]{2,1,0:T(8,128)} %param.13) | copy-start | bytes 1179652
  101.7 94.6 %all-gather.6.cloned.1.call-start = ((), (), s32[]{:S(2)}) async-start(), calls=%async_computation.4 | async-start | bytes 2359296 | tf_op jit(solution)/shard_map/all_gather | solution.py:97
  144.2 2.2 copy-start
  146.5 0.7 copy-start.6
  147.2 0.7 copy-start.7
  148.7 114.1 %all-gather.8.cloned.1.call-start = ((), (), s32[]{:S(2)}) async-start(), calls=%async_computation.5 | async-start | bytes 1769472 | tf_op jit(solution)/shard_map/all_gather | solution.py:110
  150.1 47.9 %copy-start.2 = (bf16[3,512,512]{2,1,0:T(8,128)(2,1)S(1)}, bf16[3,512,512]{2,1,0:T(8,128)(2,1)}, u32[]{:S(2)}) copy-start(bf16[3,512,512]{2,1,0:T(8,128)(2,1)} %param.15) | copy-start | bytes 4718596
  198.0 0.9 copy-start.5
  198.1 3.0 %copy-start.1 = (bf16[3,512,512]{2,1,0:T(8,128)(2,1)}, bf16[3,512,512]{2,1,0:T(8,128)(2,1)S(1)}, u32[]{:S(2)}) copy-start(bf16[3,512,512]{2,1,0:T(8,128)(2,1)S(1)} %select_dynamic-update-slice_fusion) | copy-start | bytes 4718596
  199.7 1.4 copy-start.4
Sparse Core Ops, SparseCore 0:
  11.6 77.4 reduce-scatter.1
  101.8 42.3 all-gather.3
  148.8 47.4 all-gather.5
  201.2 61.5 all-gather.7
where the time goes:
time: 273 us; the launch traced here: 272 us
  waiting for transfers between devices  232 us (85%)
  between operations  16.5 us (6%)
  local copies, waits for them, and re-layouts  10.1 us (4%)
  other arithmetic  4.88 us (2%)
  matrix products  4.75 us (2%)
  starting transfers between devices  3.57 us (1%)
    reduce_scatter x1, waiting for transfers between devices, body(): lax.psum_scatter(partial_value, 'rep', scatter_dimension=1, tiled=True)  77.7 us
    all_gather x1, waiting for transfers between devices, body(): direction = lax.all_gather(preconditioned, 'rep', axis=1, tiled=True)  61.7 us
    all_gather x1, waiting for transfers between devices, body(): fresh_whole = lax.all_gather(fresh_pair, 'rep', axis=1, tiled=True)  46.2 us
    all_gather x1, waiting for transfers between devices, body(): gathered = lax.all_gather(owned_rows, 'rep', axis=1, tiled=True)  40.6 us
    unnamed x23, local copies, waits for them, and re-layouts  6.3 us
    all_to_all x1, waiting for transfers between devices, body(): lax.all_to_all(outgoing, 'shard', split_axis=0, concat_axis=0, tiled=True)  5.91 us
  transfers between devices with their start and end apart: 5, of which 5 were waited for; matrix products, arithmetic and copies ran while one was open for 0% of the time, Pallas kernels for 0%

commit v1 on v0

--- a/solution.py
+++ b/solution.py
@@ -72,7 +72,12 @@
     owned_rows = jnp.einsum(
         "ks,src->krc", receiver, incoming, preferred_element_type=jnp.float32
     ).astype(jnp.bfloat16)
-    gathered = lax.all_gather(owned_rows, "rep", axis=1, tiled=True)
+    ring = [owned_rows]
+    for hop in range(7):
+        ring.append(lax.ppermute(ring[-1], "rep", [(dev, (dev + 1) % 8) for dev in range(8)]))
+    gathered = jnp.roll(
+        jnp.concatenate(ring[::-1], axis=1), (lax.axis_index("rep") + 1) * ring[0].shape[1], axis=1
+    )
     left_new = (
         decay_rate * left_stat
         + jnp.einsum("krc,kjc->krj", owned_rows, gathered, preferred_element_type=jnp.float32)

time: 273 us -> 296 us (1.084)
  waiting for transfers between devices: 232 us -> 251 us
    ppermute x0 -> x7, waiting for transfers between devices: none -> 63.9 us  [body(): lax.ppermute(ring[-1], 'rep', [(dev, (dev + 1) % 8) for dev in range(8)])]
    all_gather x1 -> x0, waiting for transfers between devices: 40.6 us -> none  [body(): gathered = lax.all_gather(owned_rows, 'rep', axis=1, tiled=True)]
    unnamed x23 -> x33, local copies, waits for them, and re-layouts: 6.3 us -> 7.13 us
  transfers between devices with their start and end apart: 5 -> 11, of which waited for: 5 -> 11; matrix products, arithmetic and copies ran while one was open for 0% -> 0% of each run, Pallas kernels for 0% -> 0%
where the time goes in v1:
time: 296 us; the launch traced here: 295 us
  waiting for transfers between devices  251 us (85%)
  between operations  16.6 us (6%)
  local copies, waits for them, and re-layouts  10.7 us (4%)
  other arithmetic  6.77 us (2%)
  matrix products  5 us (2%)
  starting transfers between devices  4.97 us (2%)
    reduce_scatter x1, waiting for transfers between devices, body(): lax.psum_scatter(partial_value, 'rep', scatter_dimension=1, tiled=True)  77.5 us
    ppermute x7, waiting for transfers between devices, body(): lax.ppermute(ring[-1], 'rep', [(dev, (dev + 1) % 8) for dev in range(8)])  63.9 us
    all_gather x1, waiting for transfers between devices, body(): direction = lax.all_gather(preconditioned, 'rep', axis=1, tiled=True)  60 us
    all_gather x1, waiting for transfers between devices, body(): fresh_whole = lax.all_gather(fresh_pair, 'rep', axis=1, tiled=True)  43.8 us
    unnamed x33, local copies, waits for them, and re-layouts  7.13 us
  transfers between devices with their start and end apart: 11, of which 11 were waited for; matrix products, arithmetic and copies ran while one was open for 0% of the time, Pallas kernels for 0%

profile of v1, /device:TPU:0, one launch (start us, length us, event | category | flops | bytes accessed | tf_op | source)
XLA Modules:
  0.0 295.1 jit_solution(547693028638205538)
XLA Ops:
  7.2 0.0 reduce-scatter.2.cloned.1.call-start
  7.2 2.8 copy.70
  10.0 2.1 bitcast_convert_fusion
  12.1 0.0 reduce-scatter.2.cloned.1.call-update
  12.1 0.1 reshape.53
  12.2 77.5 %reduce-scatter.2.cloned.1.call-done = f32[3,64,512]{2,1,0:T(8,128)} async-done(((f32[3,512,512]{2,1,0:T(8,128)}), f32[3,64,512]{2,1,0:T(8,128)}) %reduce-scatter.2.cloned.1.call-update) | async-done | bytes 393232 | tf_op jit(solution)/shard_map/reduce_scatter | solution.py:58
  89.7 1.0 convert_element_type.80
  90.7 0.3 fusion.96
  91.0 0.7 copy.43
  91.8 3.4 %all-to-all-start = ((bf16[4,64,512]{2,1,0:T(8,128)(2,1)}), bf16[4,64,512]{2,1,0:T(8,128)(2,1)S(1)}, u32[]{:S(2)}, u32[]{:S(2)}) async-start(bf16[4,64,512]{2,1,0:T(8,128)(2,1)} %copy.43), calls=%async_computation.1 | async-start | bytes 524288 | tf_op jit(solution)/shard_map/all_to_all | solution.py:69
  95.2 0.0 all-gather.3.cloned.1.call-start
  95.3 5.9 %all-to-all-done = bf16[4,64,512]{2,1,0:T(8,128)(2,1)S(1)} async-done(((bf16[4,64,512]{2,1,0:T(8,128)(2,1)}), bf16[4,64,512]{2,1,0:T(8,128)(2,1)S(1)}, u32[]{:S(2)}, u32[]{:S(2)}) %all-to-all-start) | async-done | bytes 262176 | tf_op jit(solution)/shard_map/all_to_all | solution.py:69
  101.2 0.4 convolution_convert_fusion.6
  101.5 1.4 collective-permute-start
  103.0 9.1 %collective-permute-done = bf16[3,64,512]{2,0,1:T(4,128)(2,1)S(1)} collective-permute-done((bf16[3,64,512]{2,0,1:T(4,128)(2,1)S(1)}, bf16[3,64,512]{2,0,1:T(4,128)(2,1)S(1)}, u32[]{:S(2)}, u32[]{:S(2)}) %collective-permute-start) | collective-permute-done | bytes 196640 | tf_op jit(solution)/shard_map/ppermute | solution.py:77
  112.0 0.0 collective-permute-start.1
  112.0 9.6 %collective-permute-done.1 = bf16[3,64,512]{2,0,1:T(4,128)(2,1)S(1)} collective-permute-done((bf16[3,64,512]{2,0,1:T(4,128)(2,1)S(1)}, bf16[3,64,512]{2,0,1:T(4,128)(2,1)S(1)}, u32[]{:S(2)}, u32[]{:S(2)}) %collective-permute-start.1) | collective-permute-done | bytes 196640 | tf_op jit(solution)/shard_map/ppermute | solution.py:77
  121.6 9.1 %collective-permute-done.2 = bf16[3,64,512]{2,0,1:T(4,128)(2,1)S(1)} collective-permute-done((bf16[3,64,512]{2,0,1:T(4,128)(2,1)S(1)}, bf16[3,64,512]{2,0,1:T(4,128)(2,1)S(1)}, u32[]{:S(2)}, u32[]{:S(2)}) %collective-permute-start.2) | collective-permute-done | bytes 196640 | tf_op jit(solution)/shard_map/ppermute | solution.py:77
  130.7 0.0 collective-permute-start.3
  130.7 9.1 %collective-permute-done.3 = bf16[3,64,512]{2,0,1:T(4,128)(2,1)S(1)} collective-permute-done((bf16[3,64,512]{2,0,1:T(4,128)(2,1)S(1)}, bf16[3,64,512]{2,0,1:T(4,128)(2,1)S(1)}, u32[]{:S(2)}, u32[]{:S(2)}) %collective-permute-start.3) | collective-permute-done | bytes 196640 | tf_op jit(solution)/shard_map/ppermute | solution.py:77
  139.8 0.0 collective-permute-start.4
  139.8 9.4 %collective-permute-done.4 = bf16[3,64,512]{2,0,1:T(4,128)(2,1)S(1)} collective-permute-done((bf16[3,64,512]{2,0,1:T(4,128)(2,1)S(1)}, bf16[3,64,512]{2,0,1:T(4,128)(2,1)S(1)}, u32[]{:S(2)}, u32[]{:S(2)}) %collective-permute-start.4) | collective-permute-done | bytes 196640 | tf_op jit(solution)/shard_map/ppermute | solution.py:77
  149.2 0.0 collective-permute-start.5
  149.2 10.5 %collective-permute-done.5 = bf16[3,64,512]{2,0,1:T(4,128)(2,1)S(1)} collective-permute-done((bf16[3,64,512]{2,0,1:T(4,128)(2,1)S(1)}, bf16[3,64,512]{2,0,1:T(4,128)(2,1)S(1)}, u32[]{:S(2)}, u32[]{:S(2)}) %collective-permute-start.5) | collective-permute-done | bytes 196640 | tf_op jit(solution)/shard_map/ppermute | solution.py:77
  159.7 0.0 collective-permute-start.6
  160.4 0.6 dynamic_slice.28
  161.6 7.1 %collective-permute-done.6 = bf16[3,64,512]{2,0,1:T(4,128)(2,1)S(1)} collective-permute-done((bf16[3,64,512]{2,0,1:T(4,128)(2,1)S(1)}, bf16[3,64,512]{2,0,1:T(4,128)(2,1)S(1)}, u32[]{:S(2)}, u32[]{:S(2)}) %collective-permute-start.6) | collective-permute-done | bytes 196640 | tf_op jit(solution)/shard_map/ppermute | solution.py:77
  168.8 0.1 constant_dynamic-update-slice_fusion.15
  168.9 0.1 constant_dynamic-update-slice_fusion.14
  169.0 0.1 constant_dynamic-update-slice_fusion.13
  169.1 0.1 constant_dynamic-update-slice_fusion.12
  169.2 0.1 constant_dynamic-update-slice_fusion.11
  169.3 0.1 constant_dynamic-update-slice_fusion.10
  169.4 0.1 constant_dynamic-update-slice_fusion.9
  169.6 0.1 constant_dynamic-update-slice_fusion.8
  169.7 0.1 constant_dynamic-update-slice_fusion.7
  169.8 0.1 constant_dynamic-update-slice_fusion.6
  169.9 0.0 copy-start.5
  169.9 0.1 constant_dynamic-update-slice_fusion.5
  170.0 0.1 constant_dynamic-update-slice_fusion.4
  170.2 0.1 constant_dynamic-update-slice_fusion.3
  170.3 0.1 constant_dynamic-update-slice_fusion.2
  170.4 0.1 constant_dynamic-update-slice_fusion.1
  170.5 0.0 copy-start.6
  170.5 0.1 constant_dynamic-update-slice_fusion
  170.6 0.7 constant_dynamic-slice_fusion.3
  171.4 0.4 constant_dynamic-slice_fusion.2
  171.8 0.7 fusion.90
  172.5 0.0 copy-start.3
  172.5 0.7 fusion.89
  173.2 0.8 pad_maximum_fusion
  174.0 0.0 all-gather.3.cloned.1.call-update
  174.0 0.0 all-gather.5.cloned.1.call-start
  175.4 0.0 copy-start.2
  175.4 43.8 %all-gather.3.cloned.1.call-done = f32[2,512,512]{2,1,0:T(8,128)} async-done(((f32[2,64,512]{2,1,0:T(8,128)}), f32[2,512,512]{2,1,0:T(8,128)}) %all-gather.3.cloned.1.call-update) | async-done | bytes 2097168 | tf_op jit(solution)/shard_map/all_gather | solution.py:102
  219.2 0.9 conditional.1
  219.2 0.8 broadcast.92
  220.1 2.0 select_dynamic-update-slice_fusion
  222.0 0.9 fusion.100
  222.9 0.0 copy-start.1
  222.9 3.0 %convolution_convert_fusion.7 = bf16[3,64,512]{2,1,0:T(8,128)(2,1)} fusion(bf16[3,512,512]{2,1,0:T(8,128)(2,1)} %select_dynamic-update-slice_fusion, bf16[3,64,512]{2,1,0:T(8,128)(2,1)S(1)} %fusion.100, bf16[3,512,512]{2,0,1:T(4,128)(2,1)S(1)} %constant_dynamic-slice_fusion.3), kind=kOutput, calls=%fused_computation.83 | convolution fusion | flops 201523200 | bytes 3538944 | tf_op jit(solution)/shard_map/kri,kic->krc/dot_general | solution.py:112
  225.9 0.0 all-gather.5.cloned.1.call-update
  226.0 60.0 %all-gather.5.cloned.1.call-done = bf16[3,512,512]{2,1,0:T(8,128)(2,1)} async-done(((bf16[3,64,512]{2,1,0:T(8,128)(2,1)}), bf16[3,512,512]{2,1,0:T(8,128)(2,1)}) %all-gather.5.cloned.1.call-update) | async-done | bytes 1572880 | tf_op jit(solution)/shard_map/all_gather | solution.py:115
  285.9 2.7 copy.71
  (16 shorter events, 0.1 us)
Async XLA Ops:
  7.2 2.8 copy-start
  7.2 82.5 %reduce-scatter.2.cloned.1.call-start = ((), (), s32[]{:S(2)}) async-start(), calls=%async_computation.2 | async-start | bytes 3538944 | tf_op jit(solution)/shard_map/reduce_scatter | solution.py:58
  10.0 2.1 copy-start.7
  91.8 9.4 %all-to-all-start = ((bf16[4,64,512]{2,1,0:T(8,128)(2,1)}), bf16[4,64,512]{2,1,0:T(8,128)(2,1)S(1)}, u32[]{:S(2)}, u32[]{:S(2)}) async-start(bf16[4,64,512]{2,1,0:T(8,128)(2,1)} %copy.43), calls=%async_computation.1 | async-start | bytes 524288 | tf_op jit(solution)/shard_map/all_to_all | solution.py:69
  95.2 124.0 %all-gather.3.cloned.1.call-start = ((), (), s32[]{:S(2)}) async-start(), calls=%async_computation.3 | async-start | bytes 2359296 | tf_op jit(solution)/shard_map/all_gather | solution.py:102
  101.5 10.5 %collective-permute-start = (bf16[3,64,512]{2,0,1:T(4,128)(2,1)S(1)}, bf16[3,64,512]{2,0,1:T(4,128)(2,1)S(1)}, u32[]{:S(2)}, u32[]{:S(2)}) collective-permute-start(bf16[3,64,512]{2,0,1:T(4,128)(2,1)S(1)} %convolution_convert_fusion.6), channel_id=1, source_target_pairs={{0,4},{4,8},{8,12},{12,16},{16,20},{20,24},{24,28},{28,0},{1,5},{5... | collective-permute-start | bytes 589832 | tf_op jit(solution)/shard_map/ppermute | solution.py:77
  112.0 9.6 %collective-permute-start.1 = (bf16[3,64,512]{2,0,1:T(4,128)(2,1)S(1)}, bf16[3,64,512]{2,0,1:T(4,128)(2,1)S(1)}, u32[]{:S(2)}, u32[]{:S(2)}) collective-permute-start(bf16[3,64,512]{2,0,1:T(4,128)(2,1)S(1)} %collective-permute-done), channel_id=1, source_target_pairs={{0,4},{4,8},{8,12},{12,16},{16,20},{20,24},{24,28},{28,0},{1,5},{5... | collective-permute-start | bytes 589832 | tf_op jit(solution)/shard_map/ppermute | solution.py:77
  121.6 9.1 %collective-permute-start.2 = (bf16[3,64,512]{2,0,1:T(4,128)(2,1)S(1)}, bf16[3,64,512]{2,0,1:T(4,128)(2,1)S(1)}, u32[]{:S(2)}, u32[]{:S(2)}) collective-permute-start(bf16[3,64,512]{2,0,1:T(4,128)(2,1)S(1)} %collective-permute-done.1), channel_id=1, source_target_pairs={{0,4},{4,8},{8,12},{12,16},{16,20},{20,24},{24,28},{28,0},{1,5},{5... | collective-permute-start | bytes 589832 | tf_op jit(solution)/shard_map/ppermute | solution.py:77
  130.7 9.1 %collective-permute-start.3 = (bf16[3,64,512]{2,0,1:T(4,128)(2,1)S(1)}, bf16[3,64,512]{2,0,1:T(4,128)(2,1)S(1)}, u32[]{:S(2)}, u32[]{:S(2)}) collective-permute-start(bf16[3,64,512]{2,0,1:T(4,128)(2,1)S(1)} %collective-permute-done.2), channel_id=1, source_target_pairs={{0,4},{4,8},{8,12},{12,16},{16,20},{20,24},{24,28},{28,0},{1,5},{5... | collective-permute-start | bytes 589832 | tf_op jit(solution)/shard_map/ppermute | solution.py:77
  139.8 9.4 %collective-permute-start.4 = (bf16[3,64,512]{2,0,1:T(4,128)(2,1)S(1)}, bf16[3,64,512]{2,0,1:T(4,128)(2,1)S(1)}, u32[]{:S(2)}, u32[]{:S(2)}) collective-permute-start(bf16[3,64,512]{2,0,1:T(4,128)(2,1)S(1)} %collective-permute-done.3), channel_id=1, source_target_pairs={{0,4},{4,8},{8,12},{12,16},{16,20},{20,24},{24,28},{28,0},{1,5},{5... | collective-permute-start | bytes 589832 | tf_op jit(solution)/shard_map/ppermute | solution.py:77
  149.2 10.5 %collective-permute-start.5 = (bf16[3,64,512]{2,0,1:T(4,128)(2,1)S(1)}, bf16[3,64,512]{2,0,1:T(4,128)(2,1)S(1)}, u32[]{:S(2)}, u32[]{:S(2)}) collective-permute-start(bf16[3,64,512]{2,0,1:T(4,128)(2,1)S(1)} %collective-permute-done.4), channel_id=1, source_target_pairs={{0,4},{4,8},{8,12},{12,16},{16,20},{20,24},{24,28},{28,0},{1,5},{5... | collective-permute-start | bytes 589832 | tf_op jit(solution)/shard_map/ppermute | solution.py:77
  159.7 9.1 %collective-permute-start.6 = (bf16[3,64,512]{2,0,1:T(4,128)(2,1)S(1)}, bf16[3,64,512]{2,0,1:T(4,128)(2,1)S(1)}, u32[]{:S(2)}, u32[]{:S(2)}) collective-permute-start(bf16[3,64,512]{2,0,1:T(4,128)(2,1)S(1)} %collective-permute-done.5), channel_id=1, source_target_pairs={{0,4},{4,8},{8,12},{12,16},{16,20},{20,24},{24,28},{28,0},{1,5},{5... | collective-permute-start | bytes 589832 | tf_op jit(solution)/shard_map/ppermute | solution.py:77
  169.9 1.9 copy-start.5
  170.5 1.9 copy-start.6
  172.5 46.7 %copy-start.3 = (f32[3,64,512]{2,1,0:T(8,128)}, f32[3,64,512]{2,1,0:T(8,128)S(1)}, u32[]{:S(2)}) copy-start(f32[3,64,512]{2,1,0:T(8,128)S(1)} %fusion.90) | copy-start | bytes 1179652
  173.2 46.0 %copy-start.4 = (f32[3,64,512]{2,1,0:T(8,128)}, f32[3,64,512]{2,1,0:T(8,128)S(1)}, u32[]{:S(2)}) copy-start(f32[3,64,512]{2,1,0:T(8,128)S(1)} %fusion.89) | copy-start | bytes 1179652
  174.0 111.9 %all-gather.5.cloned.1.call-start = ((), (), s32[]{:S(2)}) async-start(), calls=%async_computation.4 | async-start | bytes 1769472 | tf_op jit(solution)/shard_map/all_gather | solution.py:115
  175.4 46.7 %copy-start.2 = (bf16[3,64,512]{2,1,0:T(8,128)(2,1)S(1)}, bf16[3,64,512]{2,1,0:T(8,128)(2,1)}, u32[]{:S(2)}) copy-start(bf16[3,64,512]{2,1,0:T(8,128)(2,1)} %param.14) | copy-start | bytes 589828
  222.9 65.7 %copy-start.1 = (bf16[3,64,512]{2,1,0:T(8,128)(2,1)}, bf16[3,64,512]{2,1,0:T(8,128)(2,1)S(1)}, u32[]{:S(2)}) copy-start(bf16[3,64,512]{2,1,0:T(8,128)(2,1)S(1)} %fusion.100) | copy-start | bytes 589828
Sparse Core Ops, SparseCore 0:
  12.2 77.4 reduce-scatter.1
  174.1 44.9 all-gather.2
  226.1 59.8 all-gather.4
